TPU v7x, 32 devices: a whole 2x2x4 slice. The times are simulated.
32 devices in a mesh: lon: 16 (over z, y, x), lat: 2 (over core).
Axes of the slice: x: 2, y: 2, z: 4, core: 2. Of those that a mesh axis runs over, the one named last changes fastest.
Arguments:
- sketch: float32 [64, 256, 512], P(None, 'lon', 'lat'), may hold values from -6 to 6
- probe_bits: int32 [2, 256, 512], P(None, 'lon', 'lat'), may hold values from 0 to 65535
- ocean: int32 [256, 512], P('lon', 'lat'), may hold values 0 or 1
- east_cond: float32 [256, 512], P('lon', 'lat'), may hold values from 0.2 to 2
- north_cond: float32 [256, 512], P('lon', 'lat'), may hold values from 0.1 to 1
- kappa_sq: float32 [256, 512], P('lon', 'lat'), may hold values from 0.05 to 0.5
- inv_area: float32 [256, 512], P('lon', 'lat'), may hold values from 0.05 to 0.2
Outputs:
- image_out: float32 [64, 256, 512], P(None, 'lon', 'lat')
- gram_out: float32 [96, 96], replicated
Inputs may be any that keep to these rules, and one draw needn't show every extreme that they name: `probe_bits`: each word holds 16 independent sign bits, bit b of word w giving probe column 16 w + b.
All inputs are finite; a program needn't handle non-finite values. No bound on the sum of `ocean` on one device may be relied on, other than what follows from the above.
Results may differ from a plain program's by a relative error of at most 0.00015.
Values sent between devices are 32-bit elements; how exact they have to be, the bound alone decides.
No kernel may reach another device: no remote copies, remote signals or barrier semaphores. Data moves between devices by JAX's collectives and lax.ppermute only.
A program may use at most 64 MiB of HBM per device.

v0:
```python
import jax
import jax.numpy as jnp
from jax import lax
from jax.sharding import PartitionSpec as P


def padded_2(cells, sides, width, closed):
    for axis, dim in sides:
        count = lax.axis_size(axis)
        ends = count if closed else count - 1
        head = lax.slice_in_dim(cells, 0, width, axis=dim)
        tail = lax.slice_in_dim(cells, cells.shape[dim] - width, cells.shape[dim], axis=dim)
        cells = jnp.concatenate(
            [
                lax.ppermute(tail, axis, [(i, (i + 1) % count) for i in range(ends)]),
                cells,
                lax.ppermute(head, axis, [((i + 1) % count, i) for i in range(ends)]),
            ],
            axis=dim,
        )
    return cells


def sign_columns(probe_bits):
    shifts = jnp.arange(16, dtype=jnp.int32)
    picked = jnp.right_shift(probe_bits[:, None], shifts[None, :, None, None])
    flipped = jnp.bitwise_and(picked, 1)
    return (1 - 2 * flipped).astype(jnp.float32).reshape((-1,) + probe_bits.shape[1:])


def operate(padded, weights):
    middle = padded[:, 1:-1, 1:-1]
    return weights[0] * (
        weights[1] * middle
        - weights[2] * padded[:, 2:, 1:-1]
        - weights[3] * padded[:, :-2, 1:-1]
        - weights[4] * padded[:, 1:-1, 2:]
        - weights[5] * padded[:, 1:-1, :-2]
    )


def extend(field_in, thickness):
    wider = padded_2(field_in, (("lon", 1),), thickness, True)
    return padded_2(wider, (("lat", 2),), thickness, False)


def pair_gram(left, right):
    left_flat = left.reshape(left.shape[0], -1)
    right_flat = right.reshape(right.shape[0], -1)
    return jnp.einsum("ac,bc->ab", left_flat, right_flat, precision=lax.Precision.HIGHEST)


def local(sketch, probe_bits, ocean, east_cond, north_cond, kappa_sq, inv_area):
    lon_count, lat_count = ocean.shape
    sea_mask = ocean.astype(jnp.float32)
    stacked = jnp.stack([sea_mask, east_cond, north_cond, kappa_sq, inv_area])
    widened = padded_2(stacked, (("lon", 1),), 2, True)
    widened = padded_2(widened, (("lat", 2),), 2, False)
    sea_wide = widened[0]
    east_wide = widened[1]
    north_wide = widened[2]
    kappa_wide = widened[3]
    area_wide = widened[4]
    east_edges = east_wide[:-1] * sea_wide[:-1] * sea_wide[1:]
    north_edges = north_wide[:, :-1] * sea_wide[:, :-1] * sea_wide[:, 1:]
    offset = 2 - 0
    span_lon = lon_count + 2 * 0
    span_lat = lat_count + 2 * 0

    def window(array, shift_lon, shift_lat):
        return array[
            offset + shift_lon : offset + shift_lon + span_lon,
            offset + shift_lat : offset + shift_lat + span_lat,
        ]

    east_weight = window(east_edges, 0, 0)
    west_weight = window(east_edges, -1, 0)
    north_weight = window(north_edges, 0, 0)
    south_weight = window(north_edges, 0, -1)
    center_term = window(kappa_wide, 0, 0) + east_weight + west_weight + north_weight + south_weight
    interior = (
        window(sea_wide, 0, 0),
        center_term,
        east_weight,
        west_weight,
        north_weight,
        south_weight,
        window(area_wide, 0, 0),
    )
    sketch_masked = sketch * sea_mask
    columns = jnp.concatenate([sketch_masked, sign_columns(probe_bits) * sea_mask], axis=0)
    sketch_count = sketch.shape[0]
    thickness = 1
    columns_wide = extend(columns, thickness)
    first_pass = operate(columns_wide, interior)
    scaled = first_pass * interior[6]
    second = operate(extend(scaled[:sketch_count], 1), interior)
    local_gram = pair_gram(first_pass, scaled)
    summed = lax.psum(local_gram, ("lon", "lat"))
    cell_total = lax.axis_size("lon") * lon_count * lax.axis_size("lat") * lat_count
    return (second, summed / cell_total)


def solution(mesh):
    in_specs = (
        P(None, "lon", "lat"),
        P(None, "lon", "lat"),
        P("lon", "lat"),
        P("lon", "lat"),
        P("lon", "lat"),
        P("lon", "lat"),
        P("lon", "lat"),
    )
    out_specs = (P(None, "lon", "lat"), P())
    return jax.shard_map(local, mesh=mesh, in_specs=in_specs, out_specs=out_specs, check_vma=False)
```

profile of v0, /device:TPU:13, one launch (start us, length us, event | category | flops | bytes accessed | tf_op | source)
XLA Modules:
  0.0 94.8 jit_solution(9568899763508457570)
XLA Ops:
  0.6 0.7 bitcast_dynamic-update-slice_fusion.4
  1.4 0.7 bitcast_dynamic-update-slice_fusion.3
  2.1 0.7 bitcast_dynamic-update-slice_fusion.2
  2.8 0.7 bitcast_dynamic-update-slice_fusion.1
  3.5 0.7 bitcast_dynamic-update-slice_fusion
  4.3 1.3 %collective-permute-start = (f32[5,2,256]{2,1,0:T(2,128)S(1)}, f32[5,2,256]{2,1,0:T(2,128)S(1)}, u32[]{:S(2)}, u32[]{:S(2)}) collective-permute-start(f32[5,2,256]{2,1,0:T(2,128)S(1)} %get-tuple-element.20), channel_id=1, source_target_pairs={{0,2},{2,4},{4,6},{6,8},{8,10},{10,12},{12,14},{14,16},{16,18},{18... | collective-permute-start | bytes 30728 | tf_op jit(solution)/shard_map/ppermute | solution.py:15
  5.5 1.2 %collective-permute-start.1 = (f32[5,2,256]{2,1,0:T(2,128)S(1)}, f32[5,2,256]{2,1,0:T(2,128)S(1)}, u32[]{:S(2)}, u32[]{:S(2)}) collective-permute-start(f32[5,2,256]{2,1,0:T(2,128)S(1)} %get-tuple-element.21), channel_id=1, source_target_pairs={{2,0},{4,2},{6,4},{8,6},{10,8},{12,10},{14,12},{16,14},{18,16},{20... | collective-permute-start | bytes 30728 | tf_op jit(solution)/shard_map/ppermute | solution.py:17
  6.7 0.7 convert_element_type.7
  7.4 1.8 %copy_multiply_fusion = f32[64,16,256]{2,0,1:T(8,128)S(1)} fusion(f32[64,16,256]{2,1,0:T(8,128)} %param.7, f32[16,256]{1,0:T(8,128)S(1)} %convert_element_type.7), kind=kLoop, calls=%fused_computation.47 | loop fusion | flops 262144 | bytes 2113536 | tf_op jit(solution)/shard_map/mul | solution.py:90
  9.7 1.3 %collective-permute-start.2 = (f32[5,20,2]{2,1,0:T(8,128)S(1)}, f32[5,20,2]{2,1,0:T(8,128)S(1)}, u32[]{:S(2)}, u32[]{:S(2)}) collective-permute-start(f32[5,20,2]{2,1,0:T(8,128)S(1)} %get-tuple-element.18), channel_id=1, source_target_pairs={{0,1},{2,3},{4,5},{6,7},{8,9},{10,11},{12,13},{14,15},{16,17},{18,... | collective-permute-start | bytes 2408 | tf_op jit(solution)/shard_map/ppermute | solution.py:15
  11.0 3.1 %collective-permute-start.3 = (f32[5,20,2]{2,1,0:T(8,128)S(1)}, f32[5,20,2]{2,1,0:T(8,128)S(1)}, u32[]{:S(2)}, u32[]{:S(2)}) collective-permute-start(f32[5,20,2]{2,1,0:T(8,128)S(1)} %get-tuple-element.19), channel_id=1, source_target_pairs={{1,0},{3,2},{5,4},{7,6},{9,8},{11,10},{13,12},{15,14},{17,16},{19,... | collective-permute-start | bytes 2408 | tf_op jit(solution)/shard_map/ppermute | solution.py:17
  14.1 2.4 %collective-permute-start.5 = (f32[96,1,256]{2,0,1:T(8,128)S(1)}, f32[96,1,256]{2,0,1:T(8,128)S(1)}, u32[]{:S(2)}, u32[]{:S(2)}) collective-permute-start(f32[96,1,256]{2,0,1:T(8,128)S(1)} %get-tuple-element.10), channel_id=1, source_target_pairs={{0,2},{2,4},{4,6},{6,8},{8,10},{10,12},{12,14},{14,16},{16,18},{18... | collective-permute-start | bytes 294920 | tf_op jit(solution)/shard_map/ppermute | solution.py:15
  16.7 0.6 slice_bitcast_fusion.2
  17.4 0.7 slice_multiply_fusion
  18.7 0.9 collective-permute-done.5
  19.6 3.1 %collective-permute-done.4 = f32[96,1,256]{2,0,1:T(8,128)S(1)} collective-permute-done((f32[96,1,256]{2,0,1:T(8,128)S(1)}, f32[96,1,256]{2,0,1:T(8,128)S(1)}, u32[]{:S(2)}, u32[]{:S(2)}) %collective-permute-start.4) | collective-permute-done | bytes 98336 | tf_op jit(solution)/shard_map/ppermute | solution.py:17
  23.3 1.0 %copy.13 = f32[96,18,1]{0,1,2:T(8,128)} copy(f32[96,18,1]{2,0,1:T(8,128)S(1)} %get-tuple-element.6) | data formatting | bytes 13824 | tf_op jit(solution)/shard_map/slice | solution.py:11
  24.7 1.3 %collective-permute-start.7 = (f32[96,18,1]{0,1,2:T(8,128)S(1)}, f32[96,18,1]{0,1,2:T(8,128)}, u32[]{:S(2)}, u32[]{:S(2)}) collective-permute-start(f32[96,18,1]{0,1,2:T(8,128)S(1)} %copy.15), channel_id=1, source_target_pairs={{0,1},{2,3},{4,5},{6,7},{8,9},{10,11},{12,13},{14,15},{16,17},{18,... | collective-permute-start | bytes 20744 | tf_op jit(solution)/shard_map/ppermute | solution.py:15
  26.0 3.6 %collective-permute-start.6 = (f32[96,18,1]{0,1,2:T(8,128)}, f32[96,18,1]{0,1,2:T(8,128)S(1)}, u32[]{:S(2)}, u32[]{:S(2)}) collective-permute-start(f32[96,18,1]{0,1,2:T(8,128)} %copy.13), channel_id=1, source_target_pairs={{1,0},{3,2},{5,4},{7,6},{9,8},{11,10},{13,12},{15,14},{17,16},{19,... | collective-permute-start | bytes 20744 | tf_op jit(solution)/shard_map/ppermute | solution.py:17
  29.6 1.6 %fusion.29 = (f32[16,256]{1,0:T(8,128)S(1)}, f32[16,256]{1,0:T(8,128)}, f32[16,256]{1,0:T(8,128)}, f32[16,256]{1,0:T(8,128)}, f32[16,256]{1,0:T(8,128)}) fusion(f32[20,260]{1,0:T(8,128)} %get-tuple-element.14, f32[20,259]{1,0:T(8,128)} %slice_multiply_fusion, f32[19,260]{1,0:T(8,128)} %fusion.26), kind=kLoop, calls=%fused_computation.72 | loop fusion | flops 16384 | bytes 163840 | tf_op jit(solution)/shard_map/add | solution.py:80
  31.2 0.7 slice.174
  31.8 1.4 %slice.195 = f32[16,256]{1,0:T(8,128)} slice(f32[20,260]{1,0:T(8,128)} %get-tuple-element.15), slice={[2:18], [2:258]} | slice | bytes 32768 | tf_op jit(solution)/shard_map/slice | solution.py:71
  33.6 1.0 %copy.16 = f32[96,18,1]{2,0,1:T(8,128)S(1)} copy(f32[96,18,1]{0,1,2:T(8,128)} %collective-permute-done.7) | data formatting | bytes 13824 | tf_op jit(solution)/shard_map/ppermute | solution.py:15
  34.7 3.8 %broadcast_multiply_fusion = (f32[96,16,256]{2,0,1:T(8,128)S(1)}, f32[96,16,256]{2,0,1:T(8,128)S(1)}) fusion(f32[16,256]{1,0:T(8,128)} %slice.195, f32[96,1,256]{2,0,1:T(8,128)S(1)} %copy-done.1, f32[32,16,256]{2,0,1:T(8,128)S(1)} %fusion.23, f32[64,16,256]{2,0,1:T(8,128)S(1)} %copy_multiply_fusion, f32[96,1,256]{2,0,1:T(8,128)S(1)} %collective-permute-done.5, ...), kind=kLoop, calls=%fused_computation.48 | loop fusion | flops 9437184 | bytes 5043712 | tf_op jit(solution)/shard_map/mul | solution.py:96
  38.5 1.4 %collective-permute-start.9 = (f32[64,1,256]{2,0,1:T(8,128)S(1)}, f32[64,1,256]{2,0,1:T(8,128)S(1)}, u32[]{:S(2)}, u32[]{:S(2)}) collective-permute-start(f32[64,1,256]{2,0,1:T(8,128)S(1)} %get-tuple-element.8), channel_id=1, source_target_pairs={{0,2},{2,4},{4,6},{6,8},{8,10},{10,12},{12,14},{14,16},{16,18},{18... | collective-permute-start | bytes 196616 | tf_op jit(solution)/shard_map/ppermute | solution.py:15
  39.9 1.1 %collective-permute-start.8 = (f32[64,1,256]{2,0,1:T(8,128)S(1)}, f32[64,1,256]{2,0,1:T(8,128)S(1)}, u32[]{:S(2)}, u32[]{:S(2)}) collective-permute-start(f32[64,1,256]{2,0,1:T(8,128)S(1)} %get-tuple-element.9), channel_id=1, source_target_pairs={{2,0},{4,2},{6,4},{8,6},{10,8},{12,10},{14,12},{16,14},{18,16},{20... | collective-permute-start | bytes 196616 | tf_op jit(solution)/shard_map/ppermute | solution.py:17
  40.9 1.4 %convolution_bitcast_fusion = f32[96,96]{1,0:T(8,128)S(1)} fusion(f32[96,16,256]{2,0,1:T(8,128)S(1)} %get-tuple-element.5, f32[16,256]{1,0:T(8,128)S(1)} %copy-done.7), kind=kOutput, calls=%fused_computation.29 | convolution fusion | flops 453378048 | bytes 1626112 | tf_op jit(solution)/shard_map/ac,bc->ab/dot_general | solution.py:50
  42.4 42.2 %psum.7 = f32[96,96]{1,0:T(8,128)S(1)} all-reduce(f32[96,96]{1,0:T(8,128)S(1)} %convolution_bitcast_fusion), channel_id=1, replica_groups=mesh['lon'=16,'lat'=2] {'lon','lat'}, use_global_device_ids=true, to_apply=%region_0.0 | all-reduce | flops 9216 | bytes 73728 | tf_op jit(solution)/shard_map/psum | solution.py:99
  85.6 1.3 %collective-permute-start.11 = (f32[64,18,1]{0,1,2:T(8,128)S(1)}, f32[64,18,1]{0,1,2:T(8,128)S(1)}, u32[]{:S(2)}, u32[]{:S(2)}) collective-permute-start(f32[64,18,1]{0,1,2:T(8,128)S(1)} %copy.19), channel_id=1, source_target_pairs={{0,1},{2,3},{4,5},{6,7},{8,9},{10,11},{12,13},{14,15},{16,17},{18,... | collective-permute-start | bytes 13832 | tf_op jit(solution)/shard_map/ppermute | solution.py:15
  87.0 4.0 %collective-permute-start.10 = (f32[64,18,1]{0,1,2:T(8,128)S(1)}, f32[64,18,1]{0,1,2:T(8,128)S(1)}, u32[]{:S(2)}, u32[]{:S(2)}) collective-permute-start(f32[64,18,1]{0,1,2:T(8,128)S(1)} %copy.17), channel_id=1, source_target_pairs={{1,0},{3,2},{5,4},{7,6},{9,8},{11,10},{13,12},{15,14},{17,16},{19,... | collective-permute-start | bytes 13832 | tf_op jit(solution)/shard_map/ppermute | solution.py:17
  92.4 0.8 fusion.12
  93.2 1.6 %copy.21 = f32[64,16,256]{2,1,0:T(8,128)} copy(f32[64,16,256]{2,0,1:T(8,128)S(1)} %fusion.12) | data formatting | bytes 2097152
  (52 shorter events, 4.9 us)
Async XLA Ops:
  0.6 8.7 %copy-start.8 = (s32[2,16,256]{2,1,0:T(8,128)S(1)}, s32[2,16,256]{2,1,0:T(8,128)}, u32[]{:S(2)}) copy-start(s32[2,16,256]{2,1,0:T(8,128)} %param.8) | copy-start | bytes 98308
  4.3 5.3 %collective-permute-start = (f32[5,2,256]{2,1,0:T(2,128)S(1)}, f32[5,2,256]{2,1,0:T(2,128)S(1)}, u32[]{:S(2)}, u32[]{:S(2)}) collective-permute-start(f32[5,2,256]{2,1,0:T(2,128)S(1)} %get-tuple-element.20), channel_id=1, source_target_pairs={{0,2},{2,4},{4,6},{6,8},{8,10},{10,12},{12,14},{14,16},{16,18},{18... | collective-permute-start | bytes 30728 | tf_op jit(solution)/shard_map/ppermute | solution.py:15
  5.5 4.0 %collective-permute-start.1 = (f32[5,2,256]{2,1,0:T(2,128)S(1)}, f32[5,2,256]{2,1,0:T(2,128)S(1)}, u32[]{:S(2)}, u32[]{:S(2)}) collective-permute-start(f32[5,2,256]{2,1,0:T(2,128)S(1)} %get-tuple-element.21), channel_id=1, source_target_pairs={{2,0},{4,2},{6,4},{8,6},{10,8},{12,10},{14,12},{16,14},{18,16},{20... | collective-permute-start | bytes 30728 | tf_op jit(solution)/shard_map/ppermute | solution.py:17
  9.7 6.9 %collective-permute-start.2 = (f32[5,20,2]{2,1,0:T(8,128)S(1)}, f32[5,20,2]{2,1,0:T(8,128)S(1)}, u32[]{:S(2)}, u32[]{:S(2)}) collective-permute-start(f32[5,20,2]{2,1,0:T(8,128)S(1)} %get-tuple-element.18), channel_id=1, source_target_pairs={{0,1},{2,3},{4,5},{6,7},{8,9},{10,11},{12,13},{14,15},{16,17},{18,... | collective-permute-start | bytes 2408 | tf_op jit(solution)/shard_map/ppermute | solution.py:15
  11.0 5.6 %collective-permute-start.3 = (f32[5,20,2]{2,1,0:T(8,128)S(1)}, f32[5,20,2]{2,1,0:T(8,128)S(1)}, u32[]{:S(2)}, u32[]{:S(2)}) collective-permute-start(f32[5,20,2]{2,1,0:T(8,128)S(1)} %get-tuple-element.19), channel_id=1, source_target_pairs={{1,0},{3,2},{5,4},{7,6},{9,8},{11,10},{13,12},{15,14},{17,16},{19,... | collective-permute-start | bytes 2408 | tf_op jit(solution)/shard_map/ppermute | solution.py:17
  14.1 5.5 %collective-permute-start.5 = (f32[96,1,256]{2,0,1:T(8,128)S(1)}, f32[96,1,256]{2,0,1:T(8,128)S(1)}, u32[]{:S(2)}, u32[]{:S(2)}) collective-permute-start(f32[96,1,256]{2,0,1:T(8,128)S(1)} %get-tuple-element.10), channel_id=1, source_target_pairs={{0,2},{2,4},{4,6},{6,8},{8,10},{10,12},{12,14},{14,16},{16,18},{18... | collective-permute-start | bytes 294920 | tf_op jit(solution)/shard_map/ppermute | solution.py:15
  16.5 6.1 %collective-permute-start.4 = (f32[96,1,256]{2,0,1:T(8,128)S(1)}, f32[96,1,256]{2,0,1:T(8,128)S(1)}, u32[]{:S(2)}, u32[]{:S(2)}) collective-permute-start(f32[96,1,256]{2,0,1:T(8,128)S(1)} %get-tuple-element.11), channel_id=1, source_target_pairs={{2,0},{4,2},{6,4},{8,6},{10,8},{12,10},{14,12},{16,14},{18,16},{20... | collective-permute-start | bytes 294920 | tf_op jit(solution)/shard_map/ppermute | solution.py:17
  22.7 0.6 copy-start
  24.3 10.4 %copy-start.1 = (f32[96,1,256]{2,0,1:T(8,128)S(1)}, f32[96,1,256]{2,0,1:T(8,128)}, u32[]{:S(2)}) copy-start(f32[96,1,256]{2,0,1:T(8,128)} %copy-done) | copy-start | bytes 294916
  24.7 9.0 %collective-permute-start.7 = (f32[96,18,1]{0,1,2:T(8,128)S(1)}, f32[96,18,1]{0,1,2:T(8,128)}, u32[]{:S(2)}, u32[]{:S(2)}) collective-permute-start(f32[96,18,1]{0,1,2:T(8,128)S(1)} %copy.15), channel_id=1, source_target_pairs={{0,1},{2,3},{4,5},{6,7},{8,9},{10,11},{12,13},{14,15},{16,17},{18,... | collective-permute-start | bytes 20744 | tf_op jit(solution)/shard_map/ppermute | solution.py:15
  26.0 7.3 %collective-permute-start.6 = (f32[96,18,1]{0,1,2:T(8,128)}, f32[96,18,1]{0,1,2:T(8,128)S(1)}, u32[]{:S(2)}, u32[]{:S(2)}) collective-permute-start(f32[96,18,1]{0,1,2:T(8,128)} %copy.13), channel_id=1, source_target_pairs={{1,0},{3,2},{5,4},{7,6},{9,8},{11,10},{13,12},{15,14},{17,16},{19,... | collective-permute-start | bytes 20744 | tf_op jit(solution)/shard_map/ppermute | solution.py:17
  34.7 6.2 %copy-start.7 = (f32[16,256]{1,0:T(8,128)S(1)}, f32[16,256]{1,0:T(8,128)}, u32[]{:S(2)}) copy-start(f32[16,256]{1,0:T(8,128)} %slice.195) | copy-start | bytes 49156
  38.5 46.2 %collective-permute-start.9 = (f32[64,1,256]{2,0,1:T(8,128)S(1)}, f32[64,1,256]{2,0,1:T(8,128)S(1)}, u32[]{:S(2)}, u32[]{:S(2)}) collective-permute-start(f32[64,1,256]{2,0,1:T(8,128)S(1)} %get-tuple-element.8), channel_id=1, source_target_pairs={{0,2},{2,4},{4,6},{6,8},{8,10},{10,12},{12,14},{14,16},{16,18},{18... | collective-permute-start | bytes 196616 | tf_op jit(solution)/shard_map/ppermute | solution.py:15
  39.9 44.8 %collective-permute-start.8 = (f32[64,1,256]{2,0,1:T(8,128)S(1)}, f32[64,1,256]{2,0,1:T(8,128)S(1)}, u32[]{:S(2)}, u32[]{:S(2)}) collective-permute-start(f32[64,1,256]{2,0,1:T(8,128)S(1)} %get-tuple-element.9), channel_id=1, source_target_pairs={{2,0},{4,2},{6,4},{8,6},{10,8},{12,10},{14,12},{16,14},{18,16},{20... | collective-permute-start | bytes 196616 | tf_op jit(solution)/shard_map/ppermute | solution.py:17
  85.0 7.3 %copy-start.2 = (f32[16,256]{1,0:T(8,128)S(1)}, f32[16,256]{1,0:T(8,128)}, u32[]{:S(2)}) copy-start(f32[16,256]{1,0:T(8,128)} %get-tuple-element.23) | copy-start | bytes 49156
  85.0 7.3 %copy-start.3 = (f32[16,256]{1,0:T(8,128)S(1)}, f32[16,256]{1,0:T(8,128)}, u32[]{:S(2)}) copy-start(f32[16,256]{1,0:T(8,128)} %get-tuple-element.24) | copy-start | bytes 49156
  85.0 7.3 %copy-start.4 = (f32[16,256]{1,0:T(8,128)S(1)}, f32[16,256]{1,0:T(8,128)}, u32[]{:S(2)}) copy-start(f32[16,256]{1,0:T(8,128)} %get-tuple-element.25) | copy-start | bytes 49156
  85.0 7.3 %copy-start.5 = (f32[16,256]{1,0:T(8,128)S(1)}, f32[16,256]{1,0:T(8,128)}, u32[]{:S(2)}) copy-start(f32[16,256]{1,0:T(8,128)} %get-tuple-element.26) | copy-start | bytes 49156
  85.1 7.3 %copy-start.6 = (f32[16,256]{1,0:T(8,128)S(1)}, f32[16,256]{1,0:T(8,128)}, u32[]{:S(2)}) copy-start(f32[16,256]{1,0:T(8,128)} %slice.174) | copy-start | bytes 49156
  85.6 6.4 %collective-permute-start.11 = (f32[64,18,1]{0,1,2:T(8,128)S(1)}, f32[64,18,1]{0,1,2:T(8,128)S(1)}, u32[]{:S(2)}, u32[]{:S(2)}) collective-permute-start(f32[64,18,1]{0,1,2:T(8,128)S(1)} %copy.19), channel_id=1, source_target_pairs={{0,1},{2,3},{4,5},{6,7},{8,9},{10,11},{12,13},{14,15},{16,17},{18,... | collective-permute-start | bytes 13832 | tf_op jit(solution)/shard_map/ppermute | solution.py:15
  87.0 4.9 %collective-permute-start.10 = (f32[64,18,1]{0,1,2:T(8,128)S(1)}, f32[64,18,1]{0,1,2:T(8,128)S(1)}, u32[]{:S(2)}, u32[]{:S(2)}) collective-permute-start(f32[64,18,1]{0,1,2:T(8,128)S(1)} %copy.17), channel_id=1, source_target_pairs={{1,0},{3,2},{5,4},{7,6},{9,8},{11,10},{13,12},{15,14},{17,16},{19,... | collective-permute-start | bytes 13832 | tf_op jit(solution)/shard_map/ppermute | solution.py:17
where the time goes:
time: 95.8 us; the launch traced here: 94.8 us
  blocking collectives  42.2 us (44%)
  starting transfers between devices  21.9 us (23%)
  local copies, waits for them, and re-layouts  12.1 us (13%)
  other arithmetic  11.9 us (12%)
  waiting for transfers between devices  4.22 us (4%)
  matrix products  1.45 us (2%)
  between operations  0.98 us (1%)
    psum x1, blocking collectives, local(): summed = lax.psum(local_gram, ('lon', 'lat'))  42.2 us
    ppermute x6, starting transfers between devices, padded_2(): lax.ppermute(head, axis, [((i + 1) % count, i) for i in range(ends)])  13 us
    ppermute x6, starting transfers between devices, padded_2(): lax.ppermute(tail, axis, [(i, (i + 1) % count) for i in range(ends)])  8.92 us
    unnamed x23, local copies, waits for them, and re-layouts  4.01 us
    mul x1, other arithmetic, local(): scaled = first_pass * interior[6]  3.76 us
    ppermute x6, waiting for transfers between devices, padded_2(): lax.ppermute(head, axis, [((i + 1) % count, i) for i in range(ends)])  3.28 us
    slice x2, local copies, waits for them, and re-layouts, window(): array[offset + shift_lon:offset + shift_lon + span_lon, offset + shift_la...  2.12 us
  transfers between devices with their start and end apart: 12, of which 3 were waited for; matrix products, arithmetic and copies ran while one was open for 12% of the time, Pallas kernels for 0%

commit v1 on v0

--- a/solution.py
+++ b/solution.py
@@ -96,7 +96,7 @@
     scaled = first_pass * interior[6]
     second = operate(extend(scaled[:sketch_count], 1), interior)
     local_gram = pair_gram(first_pass, scaled)
-    summed = lax.psum(local_gram, ("lon", "lat"))
+    summed = lax.psum(lax.psum(local_gram, "lat"), "lon")
     cell_total = lax.axis_size("lon") * lon_count * lax.axis_size("lat") * lat_count
     return (second, summed / cell_total)
 

time: 95.8 us -> 136 us (1.42)
  the two profiles are of different devices: /device:TPU:13 before, /device:TPU:0 now
where the time goes in v1:
time: 136 us; the launch traced here: 135 us
  blocking collectives  77.5 us (57%)
  starting transfers between devices  27.7 us (20%)
  local copies, waits for them, and re-layouts  12.7 us (9%)
  other arithmetic  11.9 us (9%)
  waiting for transfers between devices  2.5 us (2%)
  matrix products  1.45 us (1%)
    psum x2, blocking collectives, local(): summed = lax.psum(lax.psum(local_gram, 'lat'), 'lon')  77.5 us
    ppermute x6, starting transfers between devices, padded_2(): lax.ppermute(head, axis, [((i + 1) % count, i) for i in range(ends)])  19.1 us
    ppermute x6, starting transfers between devices, padded_2(): lax.ppermute(tail, axis, [(i, (i + 1) % count) for i in range(ends)])  8.51 us
    unnamed x23, local copies, waits for them, and re-layouts  4.62 us
    mul x1, other arithmetic, local(): scaled = first_pass * interior[6]  3.76 us
  transfers between devices with their start and end apart: 12, of which 2 were waited for; matrix products, arithmetic and copies ran while one was open for 7% of the time, Pallas kernels for 0%

profile of v1, /device:TPU:0, one launch (start us, length us, event | category | flops | bytes accessed | tf_op | source)
XLA Modules:
  0.0 134.7 jit_solution(13255393844321951061)
XLA Ops:
  0.6 0.7 bitcast_dynamic-update-slice_fusion.4
  1.4 0.7 bitcast_dynamic-update-slice_fusion.3
  2.1 0.7 bitcast_dynamic-update-slice_fusion.2
  2.8 0.7 bitcast_dynamic-update-slice_fusion.1
  3.5 0.7 bitcast_dynamic-update-slice_fusion
  4.3 3.0 %collective-permute-start = (f32[5,2,256]{2,1,0:T(2,128)S(1)}, f32[5,2,256]{2,1,0:T(2,128)S(1)}, u32[]{:S(2)}, u32[]{:S(2)}) collective-permute-start(f32[5,2,256]{2,1,0:T(2,128)S(1)} %get-tuple-element.20), channel_id=1, source_target_pairs={{0,2},{2,4},{4,6},{6,8},{8,10},{10,12},{12,14},{14,16},{16,18},{18... | collective-permute-start | bytes 30728 | tf_op jit(solution)/shard_map/ppermute | solution.py:15
  7.3 4.1 %collective-permute-start.1 = (f32[5,2,256]{2,1,0:T(2,128)S(1)}, f32[5,2,256]{2,1,0:T(2,128)S(1)}, u32[]{:S(2)}, u32[]{:S(2)}) collective-permute-start(f32[5,2,256]{2,1,0:T(2,128)S(1)} %get-tuple-element.21), channel_id=1, source_target_pairs={{2,0},{4,2},{6,4},{8,6},{10,8},{12,10},{14,12},{16,14},{18,16},{20... | collective-permute-start | bytes 30728 | tf_op jit(solution)/shard_map/ppermute | solution.py:17
  11.3 0.7 convert_element_type.7
  12.1 1.8 %copy_multiply_fusion = f32[64,16,256]{2,0,1:T(8,128)S(1)} fusion(f32[64,16,256]{2,1,0:T(8,128)} %param.7, f32[16,256]{1,0:T(8,128)S(1)} %convert_element_type.7), kind=kLoop, calls=%fused_computation.47 | loop fusion | flops 262144 | bytes 2113536 | tf_op jit(solution)/shard_map/mul | solution.py:90
  14.3 1.5 %collective-permute-start.2 = (f32[5,20,2]{2,1,0:T(8,128)S(1)}, f32[5,20,2]{2,1,0:T(8,128)S(1)}, u32[]{:S(2)}, u32[]{:S(2)}) collective-permute-start(f32[5,20,2]{2,1,0:T(8,128)S(1)} %get-tuple-element.18), channel_id=1, source_target_pairs={{0,1},{2,3},{4,5},{6,7},{8,9},{10,11},{12,13},{14,15},{16,17},{18,... | collective-permute-start | bytes 2408 | tf_op jit(solution)/shard_map/ppermute | solution.py:15
  15.8 1.3 collective-permute-start.3
  17.2 5.6 %collective-permute-start.4 = (f32[96,1,256]{2,0,1:T(8,128)S(1)}, f32[96,1,256]{2,0,1:T(8,128)S(1)}, u32[]{:S(2)}, u32[]{:S(2)}) collective-permute-start(f32[96,1,256]{2,0,1:T(8,128)S(1)} %get-tuple-element.11), channel_id=1, source_target_pairs={{2,0},{4,2},{6,4},{8,6},{10,8},{12,10},{14,12},{16,14},{18,16},{20... | collective-permute-start | bytes 294920 | tf_op jit(solution)/shard_map/ppermute | solution.py:17
  23.0 0.6 slice_bitcast_fusion.2
  23.6 0.7 slice_multiply_fusion
  24.9 1.3 collective-permute-done.5
  26.9 1.0 copy.13
  28.3 2.6 %collective-permute-start.7 = (f32[96,18,1]{0,1,2:T(8,128)S(1)}, f32[96,18,1]{0,1,2:T(8,128)}, u32[]{:S(2)}, u32[]{:S(2)}) collective-permute-start(f32[96,18,1]{0,1,2:T(8,128)S(1)} %copy.15), channel_id=1, source_target_pairs={{0,1},{2,3},{4,5},{6,7},{8,9},{10,11},{12,13},{14,15},{16,17},{18,... | collective-permute-start | bytes 20744 | tf_op jit(solution)/shard_map/ppermute | solution.py:15
  30.9 1.3 collective-permute-start.6
  32.2 1.5 %fusion.29 = (f32[16,256]{1,0:T(8,128)S(1)}, f32[16,256]{1,0:T(8,128)}, f32[16,256]{1,0:T(8,128)}, f32[16,256]{1,0:T(8,128)}, f32[16,256]{1,0:T(8,128)}) fusion(f32[20,260]{1,0:T(8,128)} %get-tuple-element.14, f32[20,259]{1,0:T(8,128)} %slice_multiply_fusion, f32[19,260]{1,0:T(8,128)} %fusion.26), kind=kLoop, calls=%fused_computation.72 | loop fusion | flops 16384 | bytes 163840 | tf_op jit(solution)/shard_map/add | solution.py:80
  33.7 0.7 slice.174
  34.4 1.4 %slice.195 = f32[16,256]{1,0:T(8,128)} slice(f32[20,260]{1,0:T(8,128)} %get-tuple-element.15), slice={[2:18], [2:258]} | slice | bytes 32768 | tf_op jit(solution)/shard_map/slice | solution.py:71
  36.2 1.0 copy.16
  37.3 3.8 %broadcast_multiply_fusion = (f32[96,16,256]{2,0,1:T(8,128)S(1)}, f32[96,16,256]{2,0,1:T(8,128)S(1)}) fusion(f32[16,256]{1,0:T(8,128)} %slice.195, f32[96,1,256]{2,0,1:T(8,128)S(1)} %copy-done.1, f32[32,16,256]{2,0,1:T(8,128)S(1)} %fusion.23, f32[64,16,256]{2,0,1:T(8,128)S(1)} %copy_multiply_fusion, f32[96,1,256]{2,0,1:T(8,128)S(1)} %collective-permute-done.5, ...), kind=kLoop, calls=%fused_computation.48 | loop fusion | flops 9437184 | bytes 5043712 | tf_op jit(solution)/shard_map/mul | solution.py:96
  41.7 1.5 %convolution_bitcast_fusion = f32[96,96]{1,0:T(8,128)S(1)} fusion(f32[96,16,256]{2,0,1:T(8,128)S(1)} %get-tuple-element.5, f32[16,256]{1,0:T(8,128)S(1)} %copy-done.7), kind=kOutput, calls=%fused_computation.29 | convolution fusion | flops 453378048 | bytes 1626112 | tf_op jit(solution)/shard_map/ac,bc->ab/dot_general | solution.py:50
  43.3 5.6 %collective-permute-start.8 = (f32[64,1,256]{2,0,1:T(8,128)S(1)}, f32[64,1,256]{2,0,1:T(8,128)S(1)}, u32[]{:S(2)}, u32[]{:S(2)}) collective-permute-start(f32[64,1,256]{2,0,1:T(8,128)S(1)} %get-tuple-element.9), channel_id=1, source_target_pairs={{2,0},{4,2},{6,4},{8,6},{10,8},{12,10},{14,12},{16,14},{18,16},{20... | collective-permute-start | bytes 196616 | tf_op jit(solution)/shard_map/ppermute | solution.py:17
  48.9 4.1 %psum.14 = f32[96,96]{1,0:T(8,128)S(1)} all-reduce(f32[96,96]{1,0:T(8,128)S(1)} %convolution_bitcast_fusion), channel_id=1, replica_groups=mesh['lon'=16,'lat'=2] {'lat'}, use_global_device_ids=true, to_apply=%region_0.0 | all-reduce | flops 9216 | bytes 73728 | tf_op jit(solution)/shard_map/psum | solution.py:99
  53.0 73.4 %psum.15 = f32[96,96]{1,0:T(8,128)S(1)} all-reduce(f32[96,96]{1,0:T(8,128)S(1)} %psum.14), channel_id=1, replica_groups=mesh['lon'=16,'lat'=2] {'lon'}, use_global_device_ids=true, to_apply=%region_1.0 | all-reduce | flops 9216 | bytes 73728 | tf_op jit(solution)/shard_map/psum | solution.py:99
  127.4 1.3 collective-permute-start.11
  128.7 1.3 collective-permute-start.10
  130.6 1.1 collective-permute-done.10
  132.4 0.8 fusion.12
  133.2 1.6 %copy.21 = f32[64,16,256]{2,1,0:T(8,128)} copy(f32[64,16,256]{2,0,1:T(8,128)S(1)} %fusion.12) | data formatting | bytes 2097152
  (53 shorter events, 5.5 us)
Async XLA Ops:
  0.6 13.4 %copy-start.8 = (s32[2,16,256]{2,1,0:T(8,128)S(1)}, s32[2,16,256]{2,1,0:T(8,128)}, u32[]{:S(2)}) copy-start(s32[2,16,256]{2,1,0:T(8,128)} %param.8) | copy-start | bytes 98308
  4.3 9.9 %collective-permute-start = (f32[5,2,256]{2,1,0:T(2,128)S(1)}, f32[5,2,256]{2,1,0:T(2,128)S(1)}, u32[]{:S(2)}, u32[]{:S(2)}) collective-permute-start(f32[5,2,256]{2,1,0:T(2,128)S(1)} %get-tuple-element.20), channel_id=1, source_target_pairs={{0,2},{2,4},{4,6},{6,8},{8,10},{10,12},{12,14},{14,16},{16,18},{18... | collective-permute-start | bytes 30728 | tf_op jit(solution)/shard_map/ppermute | solution.py:15
  7.3 6.9 %collective-permute-start.1 = (f32[5,2,256]{2,1,0:T(2,128)S(1)}, f32[5,2,256]{2,1,0:T(2,128)S(1)}, u32[]{:S(2)}, u32[]{:S(2)}) collective-permute-start(f32[5,2,256]{2,1,0:T(2,128)S(1)} %get-tuple-element.21), channel_id=1, source_target_pairs={{2,0},{4,2},{6,4},{8,6},{10,8},{12,10},{14,12},{16,14},{18,16},{20... | collective-permute-start | bytes 30728 | tf_op jit(solution)/shard_map/ppermute | solution.py:17
  14.3 8.5 %collective-permute-start.2 = (f32[5,20,2]{2,1,0:T(8,128)S(1)}, f32[5,20,2]{2,1,0:T(8,128)S(1)}, u32[]{:S(2)}, u32[]{:S(2)}) collective-permute-start(f32[5,20,2]{2,1,0:T(8,128)S(1)} %get-tuple-element.18), channel_id=1, source_target_pairs={{0,1},{2,3},{4,5},{6,7},{8,9},{10,11},{12,13},{14,15},{16,17},{18,... | collective-permute-start | bytes 2408 | tf_op jit(solution)/shard_map/ppermute | solution.py:15
  15.8 7.0 %collective-permute-start.3 = (f32[5,20,2]{2,1,0:T(8,128)S(1)}, f32[5,20,2]{2,1,0:T(8,128)S(1)}, u32[]{:S(2)}, u32[]{:S(2)}) collective-permute-start(f32[5,20,2]{2,1,0:T(8,128)S(1)} %get-tuple-element.19), channel_id=1, source_target_pairs={{1,0},{3,2},{5,4},{7,6},{9,8},{11,10},{13,12},{15,14},{17,16},{19,... | collective-permute-start | bytes 2408 | tf_op jit(solution)/shard_map/ppermute | solution.py:17
  17.1 9.2 %collective-permute-start.5 = (f32[96,1,256]{2,0,1:T(8,128)S(1)}, f32[96,1,256]{2,0,1:T(8,128)S(1)}, u32[]{:S(2)}, u32[]{:S(2)}) collective-permute-start(f32[96,1,256]{2,0,1:T(8,128)S(1)} %get-tuple-element.10), channel_id=1, source_target_pairs={{0,2},{2,4},{4,6},{6,8},{8,10},{10,12},{12,14},{14,16},{16,18},{18... | collective-permute-start | bytes 294920 | tf_op jit(solution)/shard_map/ppermute | solution.py:15
  17.2 9.1 %collective-permute-start.4 = (f32[96,1,256]{2,0,1:T(8,128)S(1)}, f32[96,1,256]{2,0,1:T(8,128)S(1)}, u32[]{:S(2)}, u32[]{:S(2)}) collective-permute-start(f32[96,1,256]{2,0,1:T(8,128)S(1)} %get-tuple-element.11), channel_id=1, source_target_pairs={{2,0},{4,2},{6,4},{8,6},{10,8},{12,10},{14,12},{16,14},{18,16},{20... | collective-permute-start | bytes 294920 | tf_op jit(solution)/shard_map/ppermute | solution.py:17
  26.3 0.6 copy-start
  27.9 9.4 %copy-start.1 = (f32[96,1,256]{2,0,1:T(8,128)S(1)}, f32[96,1,256]{2,0,1:T(8,128)}, u32[]{:S(2)}) copy-start(f32[96,1,256]{2,0,1:T(8,128)} %copy-done) | copy-start | bytes 294916
  28.3 7.9 %collective-permute-start.7 = (f32[96,18,1]{0,1,2:T(8,128)S(1)}, f32[96,18,1]{0,1,2:T(8,128)}, u32[]{:S(2)}, u32[]{:S(2)}) collective-permute-start(f32[96,18,1]{0,1,2:T(8,128)S(1)} %copy.15), channel_id=1, source_target_pairs={{0,1},{2,3},{4,5},{6,7},{8,9},{10,11},{12,13},{14,15},{16,17},{18,... | collective-permute-start | bytes 20744 | tf_op jit(solution)/shard_map/ppermute | solution.py:15
  30.9 5.0 %collective-permute-start.6 = (f32[96,18,1]{0,1,2:T(8,128)}, f32[96,18,1]{0,1,2:T(8,128)S(1)}, u32[]{:S(2)}, u32[]{:S(2)}) collective-permute-start(f32[96,18,1]{0,1,2:T(8,128)} %copy.13), channel_id=1, source_target_pairs={{1,0},{3,2},{5,4},{7,6},{9,8},{11,10},{13,12},{15,14},{17,16},{19,... | collective-permute-start | bytes 20744 | tf_op jit(solution)/shard_map/ppermute | solution.py:17
  41.0 0.7 copy-start.7
  43.2 83.2 %collective-permute-start.9 = (f32[64,1,256]{2,0,1:T(8,128)S(1)}, f32[64,1,256]{2,0,1:T(8,128)S(1)}, u32[]{:S(2)}, u32[]{:S(2)}) collective-permute-start(f32[64,1,256]{2,0,1:T(8,128)S(1)} %get-tuple-element.8), channel_id=1, source_target_pairs={{0,2},{2,4},{4,6},{6,8},{8,10},{10,12},{12,14},{14,16},{16,18},{18... | collective-permute-start | bytes 196616 | tf_op jit(solution)/shard_map/ppermute | solution.py:15
  43.3 83.1 %collective-permute-start.8 = (f32[64,1,256]{2,0,1:T(8,128)S(1)}, f32[64,1,256]{2,0,1:T(8,128)S(1)}, u32[]{:S(2)}, u32[]{:S(2)}) collective-permute-start(f32[64,1,256]{2,0,1:T(8,128)S(1)} %get-tuple-element.9), channel_id=1, source_target_pairs={{2,0},{4,2},{6,4},{8,6},{10,8},{12,10},{14,12},{16,14},{18,16},{20... | collective-permute-start | bytes 196616 | tf_op jit(solution)/shard_map/ppermute | solution.py:17
  126.8 5.6 %copy-start.2 = (f32[16,256]{1,0:T(8,128)S(1)}, f32[16,256]{1,0:T(8,128)}, u32[]{:S(2)}) copy-start(f32[16,256]{1,0:T(8,128)} %get-tuple-element.23) | copy-start | bytes 49156
  126.8 5.6 %copy-start.3 = (f32[16,256]{1,0:T(8,128)S(1)}, f32[16,256]{1,0:T(8,128)}, u32[]{:S(2)}) copy-start(f32[16,256]{1,0:T(8,128)} %get-tuple-element.24) | copy-start | bytes 49156
  126.8 5.6 %copy-start.4 = (f32[16,256]{1,0:T(8,128)S(1)}, f32[16,256]{1,0:T(8,128)}, u32[]{:S(2)}) copy-start(f32[16,256]{1,0:T(8,128)} %get-tuple-element.25) | copy-start | bytes 49156
  126.8 5.6 %copy-start.5 = (f32[16,256]{1,0:T(8,128)S(1)}, f32[16,256]{1,0:T(8,128)}, u32[]{:S(2)}) copy-start(f32[16,256]{1,0:T(8,128)} %get-tuple-element.26) | copy-start | bytes 49156
  126.8 5.6 %copy-start.6 = (f32[16,256]{1,0:T(8,128)S(1)}, f32[16,256]{1,0:T(8,128)}, u32[]{:S(2)}) copy-start(f32[16,256]{1,0:T(8,128)} %slice.174) | copy-start | bytes 49156
  127.4 4.6 %collective-permute-start.11 = (f32[64,18,1]{0,1,2:T(8,128)S(1)}, f32[64,18,1]{0,1,2:T(8,128)S(1)}, u32[]{:S(2)}, u32[]{:S(2)}) collective-permute-start(f32[64,18,1]{0,1,2:T(8,128)S(1)} %copy.19), channel_id=1, source_target_pairs={{0,1},{2,3},{4,5},{6,7},{8,9},{10,11},{12,13},{14,15},{16,17},{18,... | collective-permute-start | bytes 13832 | tf_op jit(solution)/shard_map/ppermute | solution.py:15
  128.7 3.1 %collective-permute-start.10 = (f32[64,18,1]{0,1,2:T(8,128)S(1)}, f32[64,18,1]{0,1,2:T(8,128)S(1)}, u32[]{:S(2)}, u32[]{:S(2)}) collective-permute-start(f32[64,18,1]{0,1,2:T(8,128)S(1)} %copy.17), channel_id=1, source_target_pairs={{1,0},{3,2},{5,4},{7,6},{9,8},{11,10},{13,12},{15,14},{17,16},{19,... | collective-permute-start | bytes 13832 | tf_op jit(solution)/shard_map/ppermute | solution.py:17
